TPU v7x, 512 devices: a whole 4x4x16 slice. The times are simulated.
512 devices in a mesh: dp: 64 (over x, z), tensor: 8 (over y, core).
Axes of the slice: x: 4, y: 4, z: 16, core: 2. Of those that a mesh axis runs over, the one named last changes fastest.
Arguments:
- tokens: bfloat16 [8192, 8192], P('dp', 'tensor'), may hold values from -6 to 6
- hidden_grad: bfloat16 [8192, 28672], P('dp', 'tensor'), may hold values from -0.0625 to 0.0625
- masters: float32 [8, 64, 128, 128], P('tensor', 'dp'), may hold values from -0.5 to 0.5
- block_row: int32 [8, 32], P('tensor'), may hold values from 0 to 63, as said below
- block_col: int32 [8, 32], P('tensor'), may hold values from 0 to 27
- owners: int32 [8, 64], P('tensor'), may hold values from 0 to 63, as said below
Outputs:
- grads: float32 [8, 192, 128, 128], P('tensor', 'dp')
Inputs may be any that keep to these rules, and one draw needn't show every extreme that they name: `block_row`: in each slice the kept places are distinct. `owners`: in each slice every owner takes at most 3 of the 64 kept blocks, and some owner takes exactly 3.
All inputs are finite; a program needn't handle non-finite values.
Results may differ from a plain program's by a relative error of at most 0.0044.
Values may be sent and summed in bfloat16 or wider, within the bound.
A program may use at most 64 MiB of HBM per device.

v0:
```python
import jax
import jax.numpy as jnp
from jax import lax
from jax.sharding import PartitionSpec as P


def slot_index(owner_row, capacity):
    count_all = owner_row.shape[0]
    same_owner = owner_row[:, None] == owner_row[None, :]
    earlier = (
        jnp.arange(count_all, dtype=jnp.int32)[None, :]
        < jnp.arange(count_all, dtype=jnp.int32)[:, None]
    )
    rank_index = jnp.sum(
        jnp.logical_and(same_owner, earlier).astype(jnp.int32), axis=1, dtype=jnp.int32
    )
    return owner_row * capacity + rank_index


def column_total(part, same_column):
    return jnp.einsum("tjc,kj->tkc", part, same_column, precision=lax.Precision.HIGHEST)


def local(tokens, hidden_grad, masters, block_row, block_col, owners):
    high = lax.Precision.HIGHEST
    features = lax.all_gather(tokens, "tensor", axis=1, tiled=True)
    token_count = features.shape[0]
    block_side = masters.shape[-1]
    kept_count = block_row.shape[1]
    weights = lax.all_gather(masters.astype(jnp.bfloat16), "dp", axis=1, tiled=True)[0]
    row_index = block_row[0]
    column_index = block_col[0]
    by_block = features.reshape(token_count, features.shape[1] // block_side, block_side)
    selected = jnp.take(by_block, row_index, axis=1)
    gate_part = jnp.einsum(
        "tkb,kbc->tkc", selected, weights[:kept_count], preferred_element_type=jnp.float32
    )
    up_part = jnp.einsum(
        "tkb,kbc->tkc", selected, weights[kept_count:], preferred_element_type=jnp.float32
    )
    same_column = (column_index[:, None] == column_index[None, :]).astype(jnp.float32)
    gate_value = column_total(gate_part, same_column)
    up_value = column_total(up_part, same_column)
    grad_columns = hidden_grad.reshape(token_count, hidden_grad.shape[1] // block_side, block_side)
    upstream = jnp.take(grad_columns, column_index, axis=1).astype(jnp.float32)
    sigmoid_gate = jax.nn.sigmoid(gate_value)
    gate_grad = (
        upstream * up_value * sigmoid_gate * (1.0 + gate_value * (1.0 - sigmoid_gate))
    ).astype(jnp.bfloat16)
    up_grad = (upstream * gate_value * sigmoid_gate).astype(jnp.bfloat16)
    grad_gate = jnp.einsum("tkb,tkc->kbc", selected, gate_grad, preferred_element_type=jnp.float32)
    grad_up = jnp.einsum("tkb,tkc->kbc", selected, up_grad, preferred_element_type=jnp.float32)
    block_grads = jnp.concatenate([grad_gate, grad_up], axis=0)
    owner_count = lax.axis_size("dp")
    capacity = 3 * block_grads.shape[0] // owner_count
    slot_list = slot_index(owners[0], capacity)
    summed = lax.psum(block_grads, "dp")
    own_slots = lax.axis_index("dp") * capacity + jnp.arange(capacity, dtype=jnp.int32)
    selector = (own_slots[:, None] == slot_list[None, :]).astype(jnp.float32)
    result = jnp.einsum("sk,kbc->sbc", selector, summed, precision=high)
    return result[None]


def solution(mesh):
    return jax.shard_map(
        local,
        mesh=mesh,
        in_specs=(
            P("dp", "tensor"),
            P("dp", "tensor"),
            P("tensor", "dp", None, None),
            P("tensor", None),
            P("tensor", None),
            P("tensor", None),
        ),
        out_specs=P("tensor", "dp", None, None),
        check_vma=False,
    )
```

profile of v0, /device:TPU:8, one launch (start us, length us, event | category | flops | bytes accessed | tf_op | source)
XLA Modules:
  0.0 505.0 jit_solution(9367897133489525281)
XLA Ops:
  6.5 1.8 copy.48
  8.4 1.5 bitcast_convert_fusion
  10.0 1.6 copy.51
  11.5 0.6 copy.52
  12.2 1.6 gather_fusion.1
  13.9 31.9 %all-gather.3.cloned.1.call-done = bf16[128,8192]{0,1:T(8,128)(2,1)} async-done(((bf16[128,1024]{0,1:T(8,128)(2,1)}), bf16[128,8192]{0,1:T(8,128)(2,1)}) %all-gather.3.cloned.1.call-update) | async-done | bytes 2097168 | tf_op jit(solution)/shard_map/all_gather | solution.py:26
  45.8 3.2 copy.49
  49.1 0.7 gather_fusion
  49.8 0.6 fusion.24
  50.5 1.2 copy.61
  51.7 139.4 %all-gather.5.cloned.1.call-done = bf16[1,64,128,128]{3,2,0,1:T(8,128)(2,1)} async-done(((bf16[1,1,128,128]{3,2,0,1:T(8,128)(2,1)}), bf16[1,64,128,128]{3,2,0,1:T(8,128)(2,1)}) %all-gather.5.cloned.1.call-update) | async-done | bytes 2097168 | tf_op jit(solution)/shard_map/all_gather | solution.py:30
  191.0 1.9 convolution_bitcast_fusion
  193.0 0.5 convolution_bitcast_fusion.1
  193.5 0.7 copy-done.1
  194.2 3.5 fusion.9
  197.7 3.8 fusion.7
  201.5 0.8 fusion.22
  202.2 0.8 fusion.20
  203.0 2.5 pad_maximum_fusion
  205.5 0.6 copy-done.4
  206.1 0.2 convert_reduce_fusion
  206.3 285.7 %all-reduce.2.cloned.1.call-done = f32[64,128,128]{2,1,0:T(8,128)} async-done(((f32[64,128,128]{2,1,0:T(8,128)}), f32[64,128,128]{2,1,0:T(8,128)}) %all-reduce.2.cloned.1.call-update) | async-done | bytes 4194320 | tf_op jit(solution)/shard_map/psum | solution.py:57
  492.0 5.8 %fusion.17 = f32[1,3,128,128]{3,1,2,0:T(4,128)S(1)} fusion(f32[64,128,128]{2,1,0:T(8,128)} %all-reduce.2.cloned.1.call-done, s32[64]{0:T(128)S(1)} %fusion.40, s32[3]{0:T(128)S(1)} %iota_add_fusion), kind=kOutput, calls=%fused_computation.24 | convolution fusion | flops 37748928 | bytes 4391180 | tf_op jit(solution)/shard_map/sk,kbc->sbc/dot_general | solution.py:60
  497.8 0.7 copy.66
  (22 shorter events, 0.2 us)
Async XLA Ops:
  6.5 39.3 %all-gather.3.cloned.1.call-start = ((), (), s32[]{:S(2)}) async-start(), calls=%async_computation | async-start | bytes 2359296 | tf_op jit(solution)/shard_map/all_gather | solution.py:26
  8.3 3.8 copy-start.3
  8.4 182.7 %all-gather.5.cloned.1.call-start = ((), (), s32[]{:S(2)}) async-start(), calls=%async_computation.1 | async-start | bytes 2129920 | tf_op jit(solution)/shard_map/all_gather | solution.py:30
  9.9 482.1 %all-reduce.2.cloned.1.call-start = ((), (), s32[]{:S(2)}) async-start(), calls=%async_computation.2 | async-start | bytes 8388608 | tf_op jit(solution)/shard_map/psum | solution.py:57
  11.5 2.3 copy-start.2
  191.0 1.9 copy-start
  192.9 1.2 copy-start.1
  205.5 0.7 copy-start.4
Sparse Core Ops, SparseCore 0:
  9.5 36.2 all-gather.2
  48.8 142.2 all-gather.4
  205.6 286.3 all-reduce.1
where the time goes:
time: 505 us
  waiting for transfers between devices  457 us (90%)
  matrix products  17 us (3%)
  between operations  13.3 us (3%)
  local copies, waits for them, and re-layouts  12.8 us (3%)
    psum x1, waiting for transfers between devices, local(): summed = lax.psum(block_grads, 'dp')  286 us
    all_gather x1, waiting for transfers between devices, local(): lax.all_gather(masters.astype(jnp.bfloat16), 'dp', axis=1, tiled=True)[0]  139 us
    all_gather x1, waiting for transfers between devices, local(): features = lax.all_gather(tokens, 'tensor', axis=1, tiled=True)  31.9 us
  transfers between devices with their start and end apart: 3, of which 3 were waited for; matrix products, arithmetic and copies ran while one was open for 2% of the time, Pallas kernels for 0%

commit v1 on v0

--- a/solution.py
+++ b/solution.py
@@ -22,8 +22,21 @@
 
 
 def local(tokens, hidden_grad, masters, block_row, block_col, owners):
+
+    def push_region(values):
+        passed = jnp.concatenate(
+            lax.all_to_all(
+                jnp.stack([values for _ in range(lax.axis_size("tensor"))]),
+                axis_name="tensor",
+                split_axis=0,
+                concat_axis=0,
+            ),
+            1,
+        )
+        return passed
+
     high = lax.Precision.HIGHEST
-    features = lax.all_gather(tokens, "tensor", axis=1, tiled=True)
+    features = push_region(tokens)
     token_count = features.shape[0]
     block_side = masters.shape[-1]
     kept_count = block_row.shape[1]

time: 505 us -> 470 us (0.931)
  waiting for transfers between devices: 457 us -> 409 us
  starting transfers between devices: 0.09 us -> 9.47 us
    all_gather x1, waiting for transfers between devices: 139 us -> 103 us  [local(): lax.all_gather(masters.astype(jnp.bfloat16), 'dp', axis=1, tiled=True)[0]]
    all_gather x1 -> x0, waiting for transfers between devices: 31.9 us -> none  [local(): features = lax.all_gather(tokens, 'tensor', axis=1, tiled=True)]
    all_to_all x0 -> x1, waiting for transfers between devices: none -> 21.1 us  [push_region(): lax.all_to_all(jnp.stack([values for _ in range(lax.axis_size('tensor'))]...]
    all_to_all x0 -> x1, starting transfers between devices: none -> 9.47 us  [push_region(): lax.all_to_all(jnp.stack([values for _ in range(lax.axis_size('tensor'))]...]
  transfers between devices with their start and end apart: 3 -> 3, of which waited for: 3 -> 3; matrix products, arithmetic and copies ran while one was open for 2% -> 3% of each run, Pallas kernels for 0% -> 0%
where the time goes in v1:
time: 470 us
  waiting for transfers between devices  409 us (87%)
  matrix products  17 us (4%)
  local copies, waits for them, and re-layouts  15.6 us (3%)
  between operations  13.5 us (3%)
  starting transfers between devices  9.47 us (2%)
  other arithmetic  4.8 us (1%)
    psum x1, waiting for transfers between devices, local(): summed = lax.psum(block_grads, 'dp')  286 us
    all_gather x1, waiting for transfers between devices, local(): lax.all_gather(masters.astype(jnp.bfloat16), 'dp', axis=1, tiled=True)[0]  103 us
    all_to_all x1, waiting for transfers between devices, push_region(): lax.all_to_all(jnp.stack([values for _ in range(lax.axis_size('tensor'))]...  21.1 us
    all_to_all x1, starting transfers between devices, push_region(): lax.all_to_all(jnp.stack([values for _ in range(lax.axis_size('tensor'))]...  9.47 us
  transfers between devices with their start and end apart: 3, of which 3 were waited for; matrix products, arithmetic and copies ran while one was open for 3% of the time, Pallas kernels for 0%

profile of v1, /device:TPU:8, one launch (start us, length us, event | category | flops | bytes accessed | tf_op | source)
XLA Modules:
  0.0 469.8 jit_solution(12428547845631832805)
XLA Ops:
  6.5 1.5 bitcast_convert_fusion
  8.0 1.1 copy.34
  9.1 1.6 stack.2
  10.7 9.5 %all-to-all-start = ((bf16[8,128,1024]{1,2,0:T(8,128)(2,1)}), bf16[8,128,1024]{1,2,0:T(8,128)(2,1)S(1)}, u32[]{:S(2)}, u32[]{:S(2)}) async-start(bf16[8,128,1024]{1,2,0:T(8,128)(2,1)} %stack.2), calls=%async_computation | async-start | bytes 4194304 | tf_op jit(solution)/shard_map/all_to_all | solution.py:28
  20.2 1.3 copy.37
  21.5 1.6 copy.38
  23.1 1.6 gather_fusion.1
  24.8 21.1 %all-to-all-done = bf16[8,128,1024]{1,2,0:T(8,128)(2,1)S(1)} async-done(((bf16[8,128,1024]{1,2,0:T(8,128)(2,1)}), bf16[8,128,1024]{1,2,0:T(8,128)(2,1)S(1)}, u32[]{:S(2)}, u32[]{:S(2)}) %all-to-all-start) | async-done | bytes 2097184 | tf_op jit(solution)/shard_map/all_to_all | solution.py:28
  46.0 2.9 copy.35
  48.9 2.3 gather_fusion
  51.2 0.6 fusion.24
  51.9 1.2 copy.47
  53.0 102.6 %all-gather.2.cloned.1.call-done = bf16[1,64,128,128]{3,2,0,1:T(8,128)(2,1)} async-done(((bf16[1,1,128,128]{3,2,0,1:T(8,128)(2,1)}), bf16[1,64,128,128]{3,2,0,1:T(8,128)(2,1)}) %all-gather.2.cloned.1.call-update) | async-done | bytes 2097168 | tf_op jit(solution)/shard_map/all_gather | solution.py:43
  155.6 1.9 convolution_bitcast_fusion
  158.1 0.7 copy-done.1
  158.8 3.5 fusion.9
  162.3 3.8 fusion.7
  166.0 0.8 fusion.22
  166.8 0.8 fusion.20
  167.6 2.5 pad_maximum_fusion
  170.1 0.6 copy-done.5
  170.9 285.7 %all-reduce.2.cloned.1.call-done = f32[64,128,128]{2,1,0:T(8,128)} async-done(((f32[64,128,128]{2,1,0:T(8,128)}), f32[64,128,128]{2,1,0:T(8,128)}) %all-reduce.2.cloned.1.call-update) | async-done | bytes 4194320 | tf_op jit(solution)/shard_map/psum | solution.py:70
  456.5 5.8 %fusion.17 = f32[1,3,128,128]{3,1,2,0:T(4,128)S(1)} fusion(f32[64,128,128]{2,1,0:T(8,128)} %all-reduce.2.cloned.1.call-done, s32[64]{0:T(128)S(1)} %fusion.40, s32[3]{0:T(128)S(1)} %iota_add_fusion), kind=kOutput, calls=%fused_computation.24 | convolution fusion | flops 37748928 | bytes 4391180 | tf_op jit(solution)/shard_map/sk,kbc->sbc/dot_general | solution.py:73
  462.3 0.7 copy.52
  (24 shorter events, 0.8 us)
Async XLA Ops:
  6.5 149.1 %all-gather.2.cloned.1.call-start = ((), (), s32[]{:S(2)}) async-start(), calls=%async_computation.1 | async-start | bytes 2129920 | tf_op jit(solution)/shard_map/all_gather | solution.py:43
  10.7 9.5 %copy-start.2 = (bf16[128,3584]{1,0:T(8,128)(2,1)S(1)}, bf16[128,3584]{1,0:T(8,128)(2,1)}, u32[]{:S(2)}) copy-start(bf16[128,3584]{1,0:T(8,128)(2,1)} %param.7) | copy-start | bytes 2752516
  10.7 35.2 %all-to-all-start = ((bf16[8,128,1024]{1,2,0:T(8,128)(2,1)}), bf16[8,128,1024]{1,2,0:T(8,128)(2,1)S(1)}, u32[]{:S(2)}, u32[]{:S(2)}) async-start(bf16[8,128,1024]{1,2,0:T(8,128)(2,1)} %stack.2), calls=%async_computation | async-start | bytes 4194304 | tf_op jit(solution)/shard_map/all_to_all | solution.py:28
  20.2 2.9 copy-start.4
  20.2 436.3 %all-reduce.2.cloned.1.call-start = ((), (), s32[]{:S(2)}) async-start(), calls=%async_computation.2 | async-start | bytes 8388608 | tf_op jit(solution)/shard_map/psum | solution.py:70
  21.5 3.3 copy-start.3
  155.6 1.9 copy-start
  157.5 1.2 copy-start.1
  170.0 0.7 copy-start.5
Sparse Core Ops, SparseCore 0:
  10.3 145.2 all-gather.1
  170.2 286.3 all-reduce.1
